TPU v7x, 32 devices: a whole 2x2x4 slice. The times are simulated.
32 devices in a mesh: ctx: 8 (over z, y), grp: 2 (over core), head: 2 (over x).
Axes of the slice: x: 2, y: 2, z: 4, core: 2. Of those that a mesh axis runs over, the one named last changes fastest.
Arguments:
- residual: bfloat16 [2048, 2880], P(('ctx', 'grp')), may hold values from -10 to 10
- queries: bfloat16 [2048, 2048], P(('ctx', 'grp'), 'head'), may hold values from -32 to 32
- keys: bfloat16 [2048, 256], P(('ctx', 'grp'), 'head'), may hold values from -32 to 32
- values: bfloat16 [2048, 256], P(('ctx', 'grp'), 'head'), may hold values from -12 to 12
- out_weight: bfloat16 [2048, 2880], P('head'), may hold values from -0.125 to 0.125
- norm_gain: float32 [2880], replicated, may hold values from 0.5 to 1.5
- routes: int32 [2048, 4], P(('ctx', 'grp')), may hold values from 0 to 7, all different within a row; in each aligned block of 128 rows (0 to 127, 128 to 255, ...) at most 72 rows name the same one
- expert_weight: bfloat16 [8, 2880, 2, 1536], P('ctx', None, None, 'head'), may hold values from -0.109375 to 0.109375
Outputs:
- hidden: bfloat16 [2048, 2880], P(('ctx', 'grp'), 'head')
- active: bfloat16 [8, 2, 576, 1536], P('ctx', 'grp', None, 'head')
Inputs may be any that keep to these rules, and one draw needn't show every extreme that they name: `routes`: each token names 4 different experts; the 128 rows of one device name any one expert at most 72 times.
All inputs are finite; a program needn't handle non-finite values.
Results may differ from a plain program's by a relative error of at most 0.017.
Values may be sent and summed in bfloat16 or wider, within the bound.
A program may use at most 128 MiB of HBM per device.

v0:
```python
import functools
import jax
import jax.numpy as jnp
from jax import lax
from jax.experimental import pallas as pl
from jax.experimental.pallas import tpu as pltpu
from jax.sharding import PartitionSpec as P

D = 2880
HD = 64
TOP = 4


MESH = pl.DeviceIdType.MESH
F32 = jnp.float32
BF16 = jnp.bfloat16


def turn_of(step, count):
    return 1 + lax.rem(step + count // 2 - 1, count - 1)


def in_pair(values, group, lanes):
    zeros = jnp.zeros((values.shape[0], HD), values.dtype)
    if values.shape[1] == HD:
        return jnp.concatenate([values, zeros], 1), jnp.concatenate([zeros, values], 1)
    first = group % 2 == 0
    base = group // 2 * 2 * HD
    pair = values[:, base : base + 2 * HD]
    swapped = jnp.concatenate([pair[:, HD:], pair[:, :HD]], 1)
    low = jnp.where(lanes < HD, pair if first else swapped, jnp.zeros_like(pair))
    high = jnp.where(lanes >= HD, swapped if first else pair, jnp.zeros_like(pair))
    return low, high


def attend(block, reach, q_ref, kbuf, vbuf, att_ref):
    tokens = q_ref.shape[0]
    window = kbuf.shape[0]
    kv_local = kbuf.shape[1] // HD
    pairs = q_ref.shape[1] // (2 * HD * kv_local)
    rows = pairs * tokens
    place = lax.rem(lax.broadcasted_iota(jnp.int32, (rows, window), 0), tokens)
    column = lax.broadcasted_iota(jnp.int32, (rows, window), 1)
    ahead = place + reach * tokens - column
    allowed = (ahead >= 0) & (ahead < reach * tokens) & (column >= (reach - block) * tokens)
    lanes = lax.broadcasted_iota(jnp.int32, (window, 2 * HD), 1)
    left = lax.broadcasted_iota(jnp.int32, (rows, 2 * HD), 1) < HD
    for group in range(kv_local):
        key_pair = in_pair(kbuf[...], group, lanes)
        value_pair = in_pair(vbuf[...], group, lanes)
        first = group * pairs
        queries = jnp.concatenate(
            [
                q_ref[:, (first + p) * 2 * HD : (first + p + 1) * 2 * HD]
                for p in range(pairs)
            ],
            0,
        )
        mixed = jnp.zeros((rows, 2 * HD), F32)
        totals = []
        for side in range(2):
            scores = lax.dot_general(
                queries,
                key_pair[side],
                (((1,), (1,)), ((), ())),
                preferred_element_type=F32,
            )
            scores = jnp.where(allowed, scores * HD ** (-0.5), -1e30)
            row_max = jnp.max(scores, axis=1, keepdims=True)
            weights = jnp.where(allowed, jnp.exp(scores - row_max), 0.0)
            totals.append(jnp.sum(weights, axis=1, keepdims=True))
            mixed = mixed + jnp.dot(
                weights.astype(BF16), value_pair[side], preferred_element_type=F32
            )
        attended = (mixed / jnp.where(left, totals[0], totals[1])).astype(BF16)
        for p in range(pairs):
            att_ref[:, (first + p) * 2 * HD : (first + p + 1) * 2 * HD] = attended[
                p * tokens : (p + 1) * tokens
            ]


def layer_kernel(
    count,
    cap,
    reach,
    q_ref,
    k_ref,
    v_ref,
    res_ref,
    routes_ref,
    gain_ref,
    ow_hbm,
    w_hbm,
    hid_ref,
    act_ref,
    kbuf,
    vbuf,
    att_ref,
    ow,
    paired,
    w,
    psend,
    precv,
    hits_ref,
    before_ref,
    sbuf,
    rbuf,
    ksend_sem,
    krecv_sem,
    ow_sem,
    w_sem,
    psend_sem,
    precv_sem,
    send_sem,
    recv_sem,
    xsend_sem,
    xrecv_sem,
):
    me = lax.axis_index("ctx")
    head = lax.axis_index("head")
    heads = rbuf.shape[0]
    others = [lax.rem(head + j, heads) for j in range(1, heads)]
    half, tokens = hid_ref.shape
    width = act_ref.shape[2]

    def ow_copy(which, slot):
        rows = pl.ds(pl.multiple_of(which * half, 16), half)
        return pltpu.make_async_copy(ow_hbm.at[rows], ow.at[slot], ow_sem.at[slot])

    for j in range(1, heads):
        ow_copy(others[j - 1], j).start()
    ow_copy(head, 0).start()
    pltpu.make_async_copy(w_hbm, paired, w_sem).start()

    barrier = pltpu.get_barrier_semaphore()
    for other in others:
        pl.semaphore_signal(barrier, inc=1, device_id={"head": other}, device_id_type=MESH)

    def greet(step, carry):
        peer = lax.rem(me + step, count)
        pl.semaphore_signal(barrier, inc=1, device_id={"ctx": peer}, device_id_type=MESH)
        return carry

    lax.fori_loop(1, count, greet, 0)

    groups = lax.axis_size("grp")
    block = me * groups + lax.axis_index("grp")
    blocks = count * groups

    def at_block(index):
        return {"ctx": index // groups, "grp": lax.rem(index, groups)}

    for j in range(1, reach + 1):
        for peer in (lax.rem(block + j, blocks), lax.rem(block + blocks - j, blocks)):
            pl.semaphore_signal(barrier, inc=1, device_id=at_block(peer), device_id_type=MESH)

    def window_copies(j):
        place = pl.ds((reach - j) * tokens, tokens)
        target = at_block(lax.rem(block + j, blocks))
        return [
            pltpu.make_async_remote_copy(
                src_ref=source,
                dst_ref=buffer.at[place],
                send_sem=ksend_sem.at[n, j - 1],
                recv_sem=krecv_sem.at[n, j - 1],
                device_id=target,
                device_id_type=MESH,
            )
            for n, (source, buffer) in enumerate(((k_ref, kbuf), (v_ref, vbuf)))
        ]

    pl.semaphore_wait(barrier, count - 1 + heads - 1 + 2 * reach)
    for j in range(1, reach + 1):

        @pl.when(block + j < blocks)
        def _(j=j):
            for copy in window_copies(j):
                copy.start()

    kbuf[reach * tokens :, :] = k_ref[...]
    vbuf[reach * tokens :, :] = v_ref[...]

    def project(slot):
        return lax.dot_general(
            ow[slot], att_ref[...], (((1,), (1,)), ((), ())), preferred_element_type=F32
        ).astype(BF16)

    def exchange(j):
        return pltpu.make_async_remote_copy(
            src_ref=psend.at[j - 1],
            dst_ref=precv.at[j - 1],
            send_sem=psend_sem.at[j - 1],
            recv_sem=precv_sem.at[j - 1],
            device_id={"head": others[j - 1]},
            device_id_type=MESH,
        )

    for j in range(1, reach + 1):

        @pl.when(block >= j)
        def _(j=j):
            for copy in window_copies(j):
                copy.wait_recv()

        @pl.when(block < j)
        def _(j=j):
            place = pl.ds((reach - j) * tokens, tokens)
            kbuf[place, :] = jnp.zeros((tokens, kbuf.shape[1]), BF16)
            vbuf[place, :] = jnp.zeros((tokens, vbuf.shape[1]), BF16)

        @pl.when(block + j < blocks)
        def _(j=j):
            for copy in window_copies(j):
                copy.wait_send()

    attend(block, reach, q_ref, kbuf, vbuf, att_ref)

    for j in range(1, heads):
        ow_copy(others[j - 1], j).wait()
        psend[j - 1] = project(j)
        exchange(j).start()
    ow_copy(head, 0).wait()
    projected = project(0).astype(F32)

    expert_ids = lax.broadcasted_iota(jnp.int32, (count, tokens), 0)
    hits = jnp.zeros((count, tokens), F32)
    for k in range(routes_ref.shape[0]):
        hits = hits + jnp.where(routes_ref[k : k + 1, :] == expert_ids, 1.0, 0.0)
    earlier = jnp.where(
        lax.broadcasted_iota(jnp.int32, (tokens, tokens), 0)
        < lax.broadcasted_iota(jnp.int32, (tokens, tokens), 1),
        1.0,
        0.0,
    ).astype(BF16)
    hits_ref[...] = hits
    before_ref[...] = jnp.dot(hits.astype(BF16), earlier, preferred_element_type=F32)
    residual = res_ref[pl.ds(pl.multiple_of(head * half, 16), half), :].astype(F32)

    for j in range(1, heads):
        exchange(j).wait()
        projected = projected + precv[j - 1].astype(F32)
    hid_ref[...] = (residual + projected).astype(BF16)

    slots = lax.broadcasted_iota(jnp.int32, (cap, tokens), 0).astype(F32)

    def rows_for(expert):
        wanted = hits_ref[pl.ds(expert, 1), :] > 0.5
        picks = jnp.where((slots == before_ref[pl.ds(expert, 1), :]) & wanted, 1.0, 0.0)
        return lax.dot_general(
            picks.astype(BF16),
            hid_ref[...],
            (((1,), (1,)), ((), ())),
            preferred_element_type=F32,
        ).astype(BF16)

    def routed(step):
        turn = turn_of(step, count)
        return pltpu.make_async_remote_copy(
            src_ref=sbuf.at[turn],
            dst_ref=rbuf.at[head, me],
            send_sem=send_sem.at[turn],
            recv_sem=recv_sem.at[me],
            device_id={"ctx": lax.rem(me + turn, count)},
            device_id_type=MESH,
        )

    def landed(source):
        return pltpu.make_async_remote_copy(
            src_ref=rbuf.at[head, source],
            dst_ref=rbuf.at[head, source],
            send_sem=send_sem.at[0],
            recv_sem=recv_sem.at[source],
            device_id={"head": others[0]},
            device_id_type=MESH,
        )

    def crossed(j, source):
        return pltpu.make_async_remote_copy(
            src_ref=rbuf.at[head, source],
            dst_ref=rbuf.at[head, source],
            send_sem=xsend_sem.at[j - 1, source],
            recv_sem=xrecv_sem.at[j - 1, source],
            device_id={"head": others[j - 1]},
            device_id_type=MESH,
        )

    def cross(source):
        for j in range(1, heads):
            crossed(j, source).start()

    def mirror(source):
        for j in range(1, heads):
            origin = lax.rem(head + heads - j, heads)
            pltpu.make_async_remote_copy(
                src_ref=rbuf.at[origin, source],
                dst_ref=rbuf.at[origin, source],
                send_sem=xsend_sem.at[j - 1, source],
                recv_sem=xrecv_sem.at[j - 1, source],
                device_id={"head": others[j - 1]},
                device_id_type=MESH,
            ).wait_recv()

    def dispatch(step, carry):
        turn = turn_of(step, count)
        sbuf[turn] = rows_for(lax.rem(me + turn, count))
        routed(step).start()
        return carry

    lax.fori_loop(0, count - 1, dispatch, 0)
    rbuf[head, me] = rows_for(me)
    cross(me)
    pltpu.make_async_copy(w_hbm, paired, w_sem).wait()

    def unpair(step, carry):
        rows = pl.ds(pl.multiple_of(step * 32, 32), 32)
        pair = paired[rows]
        w[rows, :width] = pair[:, 0, :]
        w[rows, width:] = pair[:, 1, :]
        return carry

    lax.fori_loop(0, w.shape[0] // 32, unpair, 0)

    def expert(source):
        squares = jnp.zeros((cap, 1), F32)
        parts = []
        for part in range(heads):
            rows = rbuf[part, source].astype(F32)
            squares = squares + jnp.sum(rows * rows, axis=1, keepdims=True)
            parts.append((rows * gain_ref[part : part + 1, :]).astype(BF16))
        inverse_rms = lax.rsqrt(squares / (heads * half) + 1e-05)

        def product(low):
            total = jnp.zeros((cap, width), F32)
            for part in range(heads):
                total = total + jnp.dot(
                    parts[part],
                    w[part * half : (part + 1) * half, low : low + width],
                    preferred_element_type=F32,
                )
            return total

        gate = product(0) * inverse_rms
        up = product(width) * inverse_rms
        act_ref[source] = (gate * jax.nn.sigmoid(1.702 * gate) * (up + 1.0)).astype(BF16)

    def receive(step, carry):
        source = lax.rem(me + count - turn_of(step, count), count)
        landed(source).wait_recv()
        cross(source)
        before = jnp.where(
            step == 0, me, lax.rem(me + count - turn_of(jnp.maximum(step - 1, 0), count), count)
        )
        mirror(before)
        expert(before)
        return carry

    lax.fori_loop(0, count - 1, receive, 0)
    last = lax.rem(me + count - turn_of(count - 2, count), count)
    mirror(last)
    expert(last)

    def drain(step, carry):
        routed(step).wait_send()
        for j in range(1, heads):
            crossed(j, lax.rem(me + step + 1, count)).wait_send()
        return carry

    lax.fori_loop(0, count - 1, drain, 0)
    for j in range(1, heads):
        crossed(j, me).wait_send()


def body(residual, queries, keys, values, out_weight, norm_gain, routes, expert_weight):
    tokens_here = queries.shape[0]
    heads_count = lax.axis_size("head")
    reach = max(1, lax.axis_size("ctx") // 16) * lax.axis_size("grp")
    width_all = residual.shape[1]
    half = width_all // heads_count
    count = lax.axis_size("ctx")
    experts_all = expert_weight.shape[0] * count
    routed = tokens_here * TOP
    cap = min(tokens_here, routed // experts_all + max(1, routed // (8 * experts_all)))
    hidden_width = expert_weight.shape[3]
    in_vmem = pl.BlockSpec(memory_space=pltpu.VMEM)
    in_hbm = pl.BlockSpec(memory_space=pl.ANY)
    hidden, active = pl.pallas_call(
        functools.partial(layer_kernel, count, cap, reach),
        out_shape=(
            jax.ShapeDtypeStruct((half, tokens_here), BF16),
            jax.ShapeDtypeStruct((count, cap, hidden_width), BF16),
        ),
        in_specs=[in_vmem] * 6 + [in_hbm] * 2,
        out_specs=(in_vmem, in_vmem),
        scratch_shapes=[
            pltpu.VMEM(((reach + 1) * tokens_here, keys.shape[1]), BF16),
            pltpu.VMEM(((reach + 1) * tokens_here, values.shape[1]), BF16),
            pltpu.VMEM(queries.shape, BF16),
            pltpu.VMEM((heads_count, half, out_weight.shape[0]), BF16),
            pltpu.VMEM((width_all, 2, hidden_width), BF16),
            pltpu.VMEM((width_all, 2 * hidden_width), BF16),
            pltpu.VMEM((heads_count - 1, half, tokens_here), BF16),
            pltpu.VMEM((heads_count - 1, half, tokens_here), BF16),
            pltpu.VMEM((count, tokens_here), F32),
            pltpu.VMEM((count, tokens_here), F32),
            pltpu.VMEM((count, cap, half), BF16),
            pltpu.VMEM((heads_count, count, cap, half), BF16),
            pltpu.SemaphoreType.DMA((2, reach)),
            pltpu.SemaphoreType.DMA((2, reach)),
            pltpu.SemaphoreType.DMA((heads_count,)),
            pltpu.SemaphoreType.DMA,
            pltpu.SemaphoreType.DMA((heads_count - 1,)),
            pltpu.SemaphoreType.DMA((heads_count - 1,)),
            pltpu.SemaphoreType.DMA((count,)),
            pltpu.SemaphoreType.DMA((count,)),
            pltpu.SemaphoreType.DMA((heads_count - 1, count)),
            pltpu.SemaphoreType.DMA((heads_count - 1, count)),
        ],
        compiler_params=pltpu.CompilerParams(
            collective_id=0, has_side_effects=True, vmem_limit_bytes=60 * 1024 * 1024
        ),
    )(
        queries,
        keys,
        values,
        residual.T,
        routes.T,
        norm_gain.reshape(heads_count, half),
        out_weight.T,
        expert_weight[0],
    )
    return (hidden.T, active.reshape(1, 1, count * cap, hidden_width))


def solution(mesh):
    in_specs = (
        P(("ctx", "grp"), None),
        P(("ctx", "grp"), "head"),
        P(("ctx", "grp"), "head"),
        P(("ctx", "grp"), "head"),
        P("head", None),
        P(),
        P(("ctx", "grp"), None),
        P("ctx", None, None, "head"),
    )
    out_specs = (P(("ctx", "grp"), "head"), P("ctx", "grp", None, "head"))
    return jax.shard_map(body, mesh=mesh, in_specs=in_specs, out_specs=out_specs, check_vma=False)
```

profile of v0, /device:TPU:8, one launch (start us, length us, event | category | flops | bytes accessed | tf_op | source)
XLA Modules:
  0.0 90.3 jit_solution(14916469312127888489)
XLA Ops:
  0.6 1.4 %reshape.10.gain_ref = f32[2,1440]{1,0:T(2,128)} reshape(f32[2880]{0:T(1024)} %param.13) | data formatting | bytes 23040 | tf_op jit(solution)/shard_map/reshape | solution.py:427
  2.0 84.4 %shard_map.95 = (bf16[1440,128]{1,0:T(8,128)(2,1)}, bf16[8,72,768]{2,1,0:T(8,128)(2,1)}) custom-call(bf16[128,1024]{1,0:T(8,128)(2,1)} %q_ref.1, bf16[128,128]{1,0:T(8,128)(2,1)} %k_ref.1, bf16[128,128]{1,0:T(8,128)(2,1)} %v_ref.1, bf16[2880,128]{1,0:T(8,128)(2,1)} %bitcast.9, s32[4,128]{1,0:T(4,128)} %bitcast.11, f32[2,1440]{1,0:T(2,128)} %reshape.10.gain_ref, ...), custom_call_target="tpu_custom_call" | custom-call | tf_op jit(solution)/shard_map/pallas_call | solution.py:386
  86.4 1.7 %copy.12 = bf16[128,1440]{0,1:T(8,128)(2,1)} copy(bf16[128,1440]{0,1:T(8,128)(2,1)} %bitcast.10) | data formatting | bytes 737280
  88.2 2.1 %copy.13 = bf16[1,1,576,768]{3,2,1,0:T(8,128)(2,1)} copy(bf16[1,1,576,768]{3,2,1,0:T(8,128)(2,1)} %bitcast.8) | data formatting | bytes 1769472
where the time goes:
time: 90.6 us; the launch traced here: 90.3 us
  Pallas kernels  84.4 us (93%)
  local copies, waits for them, and re-layouts  5.27 us (6%)
    pallas_call x1, Pallas kernels, body(): pl.pallas_call(functools.partial(layer_kernel, count, cap, reach), out_sh...  84.4 us
    unnamed x2, local copies, waits for them, and re-layouts  3.88 us

commit v1 on v0

--- a/solution.py
+++ b/solution.py
@@ -370,6 +370,476 @@
         crossed(j, me).wait_send()
 
 
+def line_kernel(
+    count,
+    cap,
+    reach,
+    chunks,
+    q_hbm,
+    k_hbm,
+    v_hbm,
+    res_hbm,
+    routes_ref,
+    gain_ref,
+    ow_hbm,
+    w_hbm,
+    hid_hbm,
+    act_hbm,
+    q_ref,
+    kbuf,
+    vbuf,
+    res_ref,
+    att_ref,
+    ow,
+    paired,
+    w,
+    gains,
+    psend,
+    precv,
+    meta,
+    zbuf,
+    ysend,
+    rows,
+    cross,
+    acc,
+    sums,
+    out,
+    in_sem,
+    ksend_sem,
+    krecv_sem,
+    ow_sem,
+    w_sem,
+    psend_sem,
+    precv_sem,
+    msend_sem,
+    mrecv_sem,
+    zsend_sem,
+    zrecv_sem,
+    ysend_sem,
+    yrecv_sem,
+    xsend_sem,
+    xrecv_sem,
+    hid_sem,
+    out_sem,
+):
+    me = lax.axis_index("ctx")
+    head = lax.axis_index("head")
+    other = 1 - head
+    length = count // 2
+    place = me // 2
+    side = lax.rem(me, 2)
+    half, tokens = hid_hbm.shape
+    width = act_hbm.shape[2]
+    piece = half // chunks
+    groups = lax.axis_size("grp")
+    block = me * groups + lax.axis_index("grp")
+    blocks = count * groups
+
+    def at_block(index):
+        return {"ctx": index // groups, "grp": lax.rem(index, groups)}
+
+    def on_line(position):
+        return {"ctx": position * 2 + side}
+
+    partner = {"ctx": place * 2 + 1 - side}
+    across = {"head": other}
+
+    barrier = pltpu.get_barrier_semaphore()
+    peers = [on_line(lax.rem(place + j, length)) for j in range(1, length)]
+    peers += [partner, across]
+    for j in range(1, reach + 1):
+        peers += [at_block(lax.rem(block + j, blocks)), at_block(lax.rem(block + blocks - j, blocks))]
+    for peer in peers:
+        pl.semaphore_signal(barrier, inc=1, device_id=peer, device_id_type=MESH)
+
+    def own_rows(which):
+        return pl.ds(pl.multiple_of(which * half, 16), half)
+
+    mine = pl.ds(reach * tokens, tokens)
+    local = [
+        pltpu.make_async_copy(k_hbm, kbuf.at[mine], in_sem.at[0]),
+        pltpu.make_async_copy(v_hbm, vbuf.at[mine], in_sem.at[1]),
+        pltpu.make_async_copy(q_hbm, q_ref, in_sem.at[2]),
+        pltpu.make_async_copy(res_hbm.at[own_rows(head)], res_ref, in_sem.at[3]),
+    ]
+    ow_copies = [
+        pltpu.make_async_copy(ow_hbm.at[own_rows(which)], ow.at[n], ow_sem.at[n])
+        for n, which in enumerate((other, head))
+    ]
+    w_copies = [
+        pltpu.make_async_copy(w_hbm.at[own_rows(which)], paired.at[pl.ds(n * half, half)], w_sem.at[n])
+        for n, which in enumerate((head, other))
+    ]
+    for copy in local + ow_copies + w_copies:
+        copy.start()
+
+    def remote(source, target, send, recv, device):
+        return pltpu.make_async_remote_copy(
+            src_ref=source,
+            dst_ref=target,
+            send_sem=send,
+            recv_sem=recv,
+            device_id=device,
+            device_id_type=MESH,
+        )
+
+    def window_copies(j):
+        rows_at = pl.ds((reach - j) * tokens, tokens)
+        target = at_block(lax.rem(block + j, blocks))
+        return [
+            remote(source, buffer.at[rows_at], ksend_sem.at[n, j - 1], krecv_sem.at[n, j - 1], target)
+            for n, (source, buffer) in enumerate(((k_hbm, kbuf), (v_hbm, vbuf)))
+        ]
+
+    expert_ids = lax.broadcasted_iota(jnp.int32, (count, tokens), 0)
+    hits = jnp.zeros((count, tokens), F32)
+    for k in range(routes_ref.shape[0]):
+        hits = hits + jnp.where(routes_ref[k : k + 1, :] == expert_ids, 1.0, 0.0)
+    earlier = jnp.where(
+        lax.broadcasted_iota(jnp.int32, (tokens, tokens), 0)
+        < lax.broadcasted_iota(jnp.int32, (tokens, tokens), 1),
+        1.0,
+        0.0,
+    ).astype(BF16)
+    before = jnp.dot(hits.astype(BF16), earlier, preferred_element_type=F32)
+    meta[place] = jnp.where(hits > 0.5, before, -1.0)
+
+    gain = gain_ref[...]
+    low, high = gain[:, :half], gain[:, half:]
+    gains[0:1, :] = jnp.where(head == 0, low, high)
+    gains[1:2, :] = jnp.where(head == 0, high, low)
+
+    pl.semaphore_wait(barrier, len(peers))
+    for j in range(1, reach + 1):
+
+        @pl.when(block + j < blocks)
+        def _(j=j):
+            for copy in window_copies(j):
+                copy.start()
+
+    def meta_copy(j):
+        return remote(
+            meta.at[place],
+            meta.at[place],
+            msend_sem.at[j - 1],
+            mrecv_sem.at[place],
+            on_line(lax.rem(place + j, length)),
+        )
+
+    def meta_landed(j):
+        source = lax.rem(place + length - j, length)
+        return remote(
+            meta.at[source], meta.at[source], msend_sem.at[j - 1], mrecv_sem.at[source], across
+        )
+
+    for j in range(1, length):
+        meta_copy(j).start()
+
+    for j in range(1, reach + 1):
+
+        @pl.when(block < j)
+        def _(j=j):
+            rows_at = pl.ds((reach - j) * tokens, tokens)
+            kbuf[rows_at, :] = jnp.zeros((tokens, kbuf.shape[1]), BF16)
+            vbuf[rows_at, :] = jnp.zeros((tokens, vbuf.shape[1]), BF16)
+
+    for copy in local:
+        copy.wait()
+    for j in range(1, reach + 1):
+
+        @pl.when(block >= j)
+        def _(j=j):
+            for copy in window_copies(j):
+                copy.wait_recv()
+
+    attend(block, reach, q_ref, kbuf, vbuf, att_ref)
+
+    def part(index):
+        return pl.ds(index * piece, piece)
+
+    def project(slot, index):
+        return lax.dot_general(
+            ow[slot, index * piece : (index + 1) * piece, :],
+            att_ref[...],
+            (((1,), (1,)), ((), ())),
+            preferred_element_type=F32,
+        ).astype(BF16)
+
+    def exchange(index):
+        return remote(
+            psend.at[part(index)],
+            precv.at[part(index)],
+            psend_sem.at[index],
+            precv_sem.at[index],
+            across,
+        )
+
+    ow_copies[0].wait()
+    for n in range(chunks):
+        psend[n * piece : (n + 1) * piece, :] = project(0, n)
+        exchange(n).start()
+    ow_copies[1].wait()
+    for n in range(chunks):
+        span = slice(n * piece, (n + 1) * piece)
+        zbuf[place, span, :] = project(1, n)
+
+    def line_copy(owner, index, up):
+        to = jnp.where(up == 1, place + 1, place - 1)
+        spot = zbuf.at[owner, part(index)]
+        return remote(
+            spot, spot, zsend_sem.at[up, owner, index], zrecv_sem.at[owner, index], on_line(to)
+        )
+
+    def has_next(up):
+        return jnp.where(up == 1, place + 1 < length, place > 0)
+
+    for copy in w_copies:
+        copy.wait()
+
+    def unpair(step, carry):
+        at = pl.ds(pl.multiple_of(step * 32, 32), 32)
+        pair = paired[at]
+        w[at, :width] = pair[:, 0, :]
+        w[at, width:] = pair[:, 1, :]
+        return carry
+
+    lax.fori_loop(0, w.shape[0] // 32, unpair, 0)
+
+    for n in range(chunks):
+        span = slice(n * piece, (n + 1) * piece)
+        exchange(n).wait_recv()
+        total = zbuf[place, span, :].astype(F32) + precv[span, :].astype(F32)
+        zbuf[place, span, :] = (res_ref[span, :].astype(F32) + total).astype(BF16)
+        for up in range(2):
+
+            @pl.when(has_next(up))
+            def _(n=n, up=up):
+                line_copy(place, n, up).start()
+
+    hid_copy = pltpu.make_async_copy(zbuf.at[place], hid_hbm, hid_sem)
+    hid_copy.start()
+
+    for j in range(1, length):
+        meta_landed(j).wait_recv()
+
+    slots = lax.broadcasted_iota(jnp.int32, (cap, tokens), 0).astype(F32)
+
+    def y_copy(owner):
+        return remote(
+            ysend.at[owner], rows.at[owner, 1], ysend_sem.at[owner], yrecv_sem.at[owner], partner
+        )
+
+    def x_copy(owner, which):
+        return remote(
+            rows.at[owner, which],
+            cross.at[owner, which],
+            xsend_sem.at[owner, which],
+            xrecv_sem.at[owner, which],
+            across,
+        )
+
+    def pick(owner):
+        def picks(expert):
+            wanted = meta[owner, pl.ds(expert, 1), :]
+            return jnp.where(slots == wanted, 1.0, 0.0)
+
+        both = jnp.concatenate([picks(place * 2 + 1 - side), picks(me)], 0).astype(BF16)
+        found = lax.dot_general(
+            both, zbuf[owner], (((1,), (1,)), ((), ())), preferred_element_type=F32
+        )
+        ysend[owner] = found[:cap].astype(BF16)
+        y_copy(owner).start()
+        rows[owner, 0] = found[cap:].astype(BF16)
+        x_copy(owner, 0).start()
+
+    def scaled(buffer, owner, n):
+        raw = buffer[owner].astype(F32).reshape(2 * cap, half)
+        squares = jnp.sum(raw * raw, axis=1, keepdims=True)
+        return squares, (raw * gains[n : n + 1, :]).astype(BF16)
+
+    def first(owner):
+        squares, left = scaled(rows, owner, 0)
+        sums[owner] = jnp.broadcast_to(squares, (2 * cap, sums.shape[2]))
+        for low in (0, width):
+            acc[owner, :, low : low + width] = jnp.dot(
+                left, w[:half, low : low + width], preferred_element_type=F32
+            )
+
+    def result(owner, which):
+        source = owner * 2 + jnp.where(which == 0, side, 1 - side)
+        return pltpu.make_async_copy(out.at[owner, which], act_hbm.at[source], out_sem.at[owner, which])
+
+    def second(owner):
+        squares, right = scaled(cross, owner, 1)
+        squares = squares + sums[owner][:, :1]
+        inverse_rms = lax.rsqrt(squares / (2 * half) + 1e-05)
+
+        def product(low):
+            return (
+                acc[owner, :, low : low + width]
+                + jnp.dot(right, w[half:, low : low + width], preferred_element_type=F32)
+            ) * inverse_rms
+
+        gate = product(0)
+        up = product(width)
+        active = gate * jax.nn.sigmoid(1.702 * gate) * (up + 1.0)
+        out[owner] = active.reshape(2, cap, width).astype(BF16)
+        for which in range(2):
+            result(owner, which).start()
+
+    def owner_of(step, up):
+        return jnp.where(up == 1, place + step, place - step)
+
+    def exists(step, up):
+        owner = owner_of(step, up)
+        return (owner >= 0) & (owner < length) & (step + 1 - up > 0)
+
+    def each(step, action):
+        def one(up, carry):
+            @pl.when(exists(step, up))
+            def _():
+                action(owner_of(step, up), up)
+
+            return carry
+
+        lax.fori_loop(0, 2, one, 0)
+
+    def arrive(owner, up):
+        @pl.when(owner != place)
+        def _():
+            for n in range(chunks):
+                line_copy(owner, n, 1 - up).wait_recv()
+
+                @pl.when(has_next(1 - up))
+                def _(n=n):
+                    line_copy(owner, n, 1 - up).start()
+
+    def meet(owner, up):
+        y_copy(owner).wait_recv()
+        x_copy(owner, 1).start()
+        first(owner)
+
+    def finish(owner, up):
+        for which in range(2):
+            x_copy(owner, which).wait_recv()
+        second(owner)
+
+    def advance(step, carry):
+        each(step, arrive)
+        each(step, lambda owner, up: pick(owner))
+
+        @pl.when(step > 0)
+        def _():
+            each(step - 1, finish)
+
+        each(step, meet)
+        return carry
+
+    lax.fori_loop(0, length, advance, 0)
+    each(length - 1, finish)
+
+    def drain(owner, carry):
+        y_copy(owner).wait_send()
+        for which in range(2):
+            x_copy(owner, which).wait_send()
+            result(owner, which).wait()
+        for n in range(chunks):
+            for up in range(2):
+                came = jnp.where(up == 1, owner <= place, owner >= place)
+
+                @pl.when(has_next(up) & came)
+                def _(n=n, up=up):
+                    line_copy(owner, n, up).wait_send()
+
+        return carry
+
+    lax.fori_loop(0, length, drain, 0)
+    hid_copy.wait()
+    for j in range(1, length):
+        meta_copy(j).wait_send()
+    for n in range(chunks):
+        exchange(n).wait_send()
+    for j in range(1, reach + 1):
+
+        @pl.when(block + j < blocks)
+        def _(j=j):
+            for copy in window_copies(j):
+                copy.wait_send()
+
+
+def along_line(
+    count, cap, reach, queries, keys, values, residual, routes, norm_gain, out_weight, expert_weight
+):
+    tokens = queries.shape[0]
+    width_all = residual.shape[1]
+    half = width_all // 2
+    length = count // 2
+    width = expert_weight.shape[3]
+    chunks = max(n for n in range(1, 4) if half % (16 * n) == 0)
+    in_vmem = pl.BlockSpec(memory_space=pltpu.VMEM)
+    in_hbm = pl.BlockSpec(memory_space=pl.ANY)
+    dma = pltpu.SemaphoreType.DMA
+    return pl.pallas_call(
+        functools.partial(line_kernel, count, cap, reach, chunks),
+        out_shape=(
+            jax.ShapeDtypeStruct((half, tokens), BF16),
+            jax.ShapeDtypeStruct((count, cap, width), BF16),
+        ),
+        in_specs=[in_hbm] * 4 + [in_vmem] * 2 + [in_hbm] * 2,
+        out_specs=(in_hbm, in_hbm),
+        scratch_shapes=[
+            pltpu.VMEM(queries.shape, BF16),
+            pltpu.VMEM(((reach + 1) * tokens, keys.shape[1]), BF16),
+            pltpu.VMEM(((reach + 1) * tokens, values.shape[1]), BF16),
+            pltpu.VMEM((half, tokens), BF16),
+            pltpu.VMEM(queries.shape, BF16),
+            pltpu.VMEM((2, half, out_weight.shape[0]), BF16),
+            pltpu.VMEM((width_all, 2, width), BF16),
+            pltpu.VMEM((width_all, 2 * width), BF16),
+            pltpu.VMEM((2, half), F32),
+            pltpu.VMEM((half, tokens), BF16),
+            pltpu.VMEM((half, tokens), BF16),
+            pltpu.VMEM((length, count, tokens), F32),
+            pltpu.VMEM((length, half, tokens), BF16),
+            pltpu.VMEM((length, cap, half), BF16),
+            pltpu.VMEM((length, 2, cap, half), BF16),
+            pltpu.VMEM((length, 2, cap, half), BF16),
+            pltpu.VMEM((length, 2 * cap, 2 * width), F32),
+            pltpu.VMEM((length, 2 * cap, 128), F32),
+            pltpu.VMEM((length, 2, cap, width), BF16),
+            dma((4,)),
+            dma((2, reach)),
+            dma((2, reach)),
+            dma((2,)),
+            dma((2,)),
+            dma((chunks,)),
+            dma((chunks,)),
+            dma((length - 1,)),
+            dma((length,)),
+            dma((2, length, chunks)),
+            dma((length, chunks)),
+            dma((length,)),
+            dma((length,)),
+            dma((length, 2)),
+            dma((length, 2)),
+            dma,
+            dma((length, 2)),
+        ],
+        compiler_params=pltpu.CompilerParams(
+            collective_id=1, has_side_effects=True, vmem_limit_bytes=60 * 1024 * 1024
+        ),
+    )(
+        queries,
+        keys,
+        values,
+        residual.T,
+        routes.T,
+        norm_gain.reshape(1, width_all),
+        out_weight.T,
+        expert_weight[0],
+    )
+
+
 def body(residual, queries, keys, values, out_weight, norm_gain, routes, expert_weight):
     tokens_here = queries.shape[0]
     heads_count = lax.axis_size("head")
@@ -381,6 +851,21 @@
     routed = tokens_here * TOP
     cap = min(tokens_here, routed // experts_all + max(1, routed // (8 * experts_all)))
     hidden_width = expert_weight.shape[3]
+    if heads_count == 2 and count % 2 == 0 and experts_all == count and 2 * cap >= tokens_here:
+        hidden, active = along_line(
+            count,
+            cap,
+            reach,
+            queries,
+            keys,
+            values,
+            residual,
+            routes,
+            norm_gain,
+            out_weight,
+            expert_weight,
+        )
+        return (hidden.T, active.reshape(1, 1, count * cap, hidden_width))
     in_vmem = pl.BlockSpec(memory_space=pltpu.VMEM)
     in_hbm = pl.BlockSpec(memory_space=pl.ANY)
     hidden, active = pl.pallas_call(

time: 90.6 us -> 83.8 us (0.925)
  the two profiles are of different devices: /device:TPU:8 before, /device:TPU:0 now
where the time goes in v1:
time: 83.8 us; the launch traced here: 83.5 us
  Pallas kernels  77.7 us (93%)
  local copies, waits for them, and re-layouts  5.2 us (6%)
    pallas_call x1, Pallas kernels, along_line(): pl.pallas_call(functools.partial(line_kernel, count, cap, reach, chunks),...  77.7 us
    unnamed x2, local copies, waits for them, and re-layouts  3.88 us

profile of v1, /device:TPU:0, one launch (start us, length us, event | category | flops | bytes accessed | tf_op | source)
XLA Modules:
  0.0 83.5 jit_solution(17179754535466048235)
XLA Ops:
  0.6 1.3 %reshape.10.gain_ref = f32[1,2880]{1,0:T(1,128)} reshape(f32[2880]{0:T(1024)} %param.13) | data formatting | bytes 23040 | tf_op jit(solution)/shard_map/reshape | solution.py:837
  1.9 77.7 %shard_map.95 = (bf16[1440,128]{1,0:T(8,128)(2,1)}, bf16[8,72,768]{2,1,0:T(8,128)(2,1)}) custom-call(bf16[128,1024]{1,0:T(8,128)(2,1)} %q_hbm.1, bf16[128,128]{1,0:T(8,128)(2,1)} %k_hbm.1, bf16[128,128]{1,0:T(8,128)(2,1)} %v_hbm.1, bf16[2880,128]{1,0:T(8,128)(2,1)} %bitcast.9, s32[4,128]{1,0:T(4,128)} %bitcast.11, f32[1,2880]{1,0:T(1,128)} %reshape.10.gain_ref, ...), custom_call_target="tpu_custom_call" | custom-call | tf_op jit(solution)/shard_map/pallas_call | solution.py:782
  79.6 1.7 %copy.12 = bf16[128,1440]{0,1:T(8,128)(2,1)} copy(bf16[128,1440]{0,1:T(8,128)(2,1)} %bitcast.10) | data formatting | bytes 737280
  81.4 2.1 %copy.13 = bf16[1,1,576,768]{3,2,1,0:T(8,128)(2,1)} copy(bf16[1,1,576,768]{3,2,1,0:T(8,128)(2,1)} %bitcast.8) | data formatting | bytes 1769472

commit v2 on v1

--- a/solution.py
+++ b/solution.py
@@ -313,9 +313,9 @@
 
     def unpair(step, carry):
         rows = pl.ds(pl.multiple_of(step * 32, 32), 32)
-        pair = paired[rows]
-        w[rows, :width] = pair[:, 0, :]
-        w[rows, width:] = pair[:, 1, :]
+        pair = jnp.swapaxes(paired[rows], 0, 1)
+        w[rows, :width] = pair[0]
+        w[rows, width:] = pair[1]
         return carry
 
     lax.fori_loop(0, w.shape[0] // 32, unpair, 0)
@@ -598,9 +598,9 @@
 
     def unpair(step, carry):
         at = pl.ds(pl.multiple_of(step * 32, 32), 32)
-        pair = paired[at]
-        w[at, :width] = pair[:, 0, :]
-        w[at, width:] = pair[:, 1, :]
+        pair = jnp.swapaxes(paired[at], 0, 1)
+        w[at, :width] = pair[0]
+        w[at, width:] = pair[1]
         return carry
 
     lax.fori_loop(0, w.shape[0] // 32, unpair, 0)
@@ -735,8 +735,7 @@
         each(step, meet)
         return carry
 
-    lax.fori_loop(0, length, advance, 0)
-    each(length - 1, finish)
+    lax.fori_loop(0, length + 1, advance, 0)
 
     def drain(owner, carry):
         y_copy(owner).wait_send()

time: 83.8 us -> 70.8 us (0.84)
  Pallas kernels: 77.7 us -> 64.6 us
    pallas_call x1, Pallas kernels: 77.7 us -> 64.6 us  [along_line(): pl.pallas_call(functools.partial(line_kernel, count, cap, reach, chunks),...]
where the time goes in v2:
time: 70.8 us; the launch traced here: 70.5 us
  Pallas kernels  64.6 us (91%)
  local copies, waits for them, and re-layouts  5.2 us (7%)
    pallas_call x1, Pallas kernels, along_line(): pl.pallas_call(functools.partial(line_kernel, count, cap, reach, chunks),...  64.6 us
    unnamed x2, local copies, waits for them, and re-layouts  3.88 us

profile of v2, /device:TPU:0, one launch (start us, length us, event | category | flops | bytes accessed | tf_op | source)
XLA Modules:
  0.0 70.5 jit_solution(15193261973158205334)
XLA Ops:
  0.6 1.3 %reshape.10.gain_ref = f32[1,2880]{1,0:T(1,128)} reshape(f32[2880]{0:T(1024)} %param.13) | data formatting | bytes 23040 | tf_op jit(solution)/shard_map/reshape | solution.py:836
  1.9 64.6 %shard_map.95 = (bf16[1440,128]{1,0:T(8,128)(2,1)}, bf16[8,72,768]{2,1,0:T(8,128)(2,1)}) custom-call(bf16[128,1024]{1,0:T(8,128)(2,1)} %q_hbm.1, bf16[128,128]{1,0:T(8,128)(2,1)} %k_hbm.1, bf16[128,128]{1,0:T(8,128)(2,1)} %v_hbm.1, bf16[2880,128]{1,0:T(8,128)(2,1)} %bitcast.9, s32[4,128]{1,0:T(4,128)} %bitcast.11, f32[1,2880]{1,0:T(1,128)} %reshape.10.gain_ref, ...), custom_call_target="tpu_custom_call" | custom-call | tf_op jit(solution)/shard_map/pallas_call | solution.py:781
  66.6 1.7 %copy.12 = bf16[128,1440]{0,1:T(8,128)(2,1)} copy(bf16[128,1440]{0,1:T(8,128)(2,1)} %bitcast.10) | data formatting | bytes 737280
  68.3 2.1 %copy.13 = bf16[1,1,576,768]{3,2,1,0:T(8,128)(2,1)} copy(bf16[1,1,576,768]{3,2,1,0:T(8,128)(2,1)} %bitcast.8) | data formatting | bytes 1769472

commit v3 on v2

--- a/solution.py
+++ b/solution.py
@@ -374,7 +374,8 @@
     count,
     cap,
     reach,
-    chunks,
+    late,
+    early,
     q_hbm,
     k_hbm,
     v_hbm,
@@ -430,7 +431,9 @@
     side = lax.rem(me, 2)
     half, tokens = hid_hbm.shape
     width = act_hbm.shape[2]
-    piece = half // chunks
+    own_parts = late + early
+    parts = own_parts + early
+    piece = half // own_parts
     groups = lax.axis_size("grp")
     block = me * groups + lax.axis_index("grp")
     blocks = count * groups
@@ -452,25 +455,39 @@
     for peer in peers:
         pl.semaphore_signal(barrier, inc=1, device_id=peer, device_id_type=MESH)
 
-    def own_rows(which):
-        return pl.ds(pl.multiple_of(which * half, 16), half)
+    def span(which, start, stop):
+        return pl.ds(pl.multiple_of(which * half + start * piece, 16), (stop - start) * piece)
 
     mine = pl.ds(reach * tokens, tokens)
+    own_spot = pl.ds(0, half)
+    early_spot = pl.ds(half, early * piece)
+    late_spot = pl.ds(parts * piece, late * piece)
     local = [
         pltpu.make_async_copy(k_hbm, kbuf.at[mine], in_sem.at[0]),
         pltpu.make_async_copy(v_hbm, vbuf.at[mine], in_sem.at[1]),
         pltpu.make_async_copy(q_hbm, q_ref, in_sem.at[2]),
-        pltpu.make_async_copy(res_hbm.at[own_rows(head)], res_ref, in_sem.at[3]),
+    ]
+    res_copies = [
+        pltpu.make_async_copy(res_hbm.at[span(head, 0, own_parts)], res_ref.at[own_spot], in_sem.at[3]),
+        pltpu.make_async_copy(
+            res_hbm.at[span(other, late, own_parts)], res_ref.at[early_spot], in_sem.at[4]
+        ),
+    ]
+    w_copies = [
+        pltpu.make_async_copy(w_hbm.at[span(which, low, high)], paired.at[spot], w_sem.at[n])
+        for n, (which, low, high, spot) in enumerate(
+            (
+                (head, 0, own_parts, own_spot),
+                (other, late, own_parts, early_spot),
+                (other, 0, late, late_spot),
+            )
+        )
     ]
     ow_copies = [
-        pltpu.make_async_copy(ow_hbm.at[own_rows(which)], ow.at[n], ow_sem.at[n])
+        pltpu.make_async_copy(ow_hbm.at[span(which, 0, own_parts)], ow.at[n], ow_sem.at[n])
         for n, which in enumerate((other, head))
     ]
-    w_copies = [
-        pltpu.make_async_copy(w_hbm.at[own_rows(which)], paired.at[pl.ds(n * half, half)], w_sem.at[n])
-        for n, which in enumerate((head, other))
-    ]
-    for copy in local + ow_copies + w_copies:
+    for copy in local + w_copies + ow_copies + res_copies:
         copy.start()
 
     def remote(source, target, send, recv, device):
@@ -504,10 +521,13 @@
     before = jnp.dot(hits.astype(BF16), earlier, preferred_element_type=F32)
     meta[place] = jnp.where(hits > 0.5, before, -1.0)
 
-    gain = gain_ref[...]
-    low, high = gain[:, :half], gain[:, half:]
-    gains[0:1, :] = jnp.where(head == 0, low, high)
-    gains[1:2, :] = jnp.where(head == 0, high, low)
+    gain = gain_ref[...].reshape(1, 2 * half)
+    order = [(0, n) for n in range(own_parts)]
+    order += [(1, n) for n in range(late, own_parts)] + [(1, n) for n in range(late)]
+    for n, (far, index) in enumerate(order):
+        left = gain[:, index * piece : (index + 1) * piece]
+        right = gain[:, half + index * piece : half + (index + 1) * piece]
+        gains[n : n + 1, :] = jnp.where(head == far, left, right)
 
     pl.semaphore_wait(barrier, len(peers))
     for j in range(1, reach + 1):
@@ -535,6 +555,18 @@
     for j in range(1, length):
         meta_copy(j).start()
 
+    for copy in w_copies:
+        copy.wait()
+
+    def unpair(step, carry):
+        at = pl.ds(pl.multiple_of(step * 32, 32), 32)
+        pair = jnp.swapaxes(paired[at], 0, 1)
+        w[at, :width] = pair[0]
+        w[at, width:] = pair[1]
+        return carry
+
+    lax.fori_loop(0, w.shape[0] // 32, unpair, 0)
+
     for j in range(1, reach + 1):
 
         @pl.when(block < j)
@@ -555,11 +587,11 @@
     attend(block, reach, q_ref, kbuf, vbuf, att_ref)
 
     def part(index):
-        return pl.ds(index * piece, piece)
+        return pl.ds(pl.multiple_of(index * piece, 16), piece)
 
     def project(slot, index):
         return lax.dot_general(
-            ow[slot, index * piece : (index + 1) * piece, :],
+            ow[slot, part(index), :],
             att_ref[...],
             (((1,), (1,)), ((), ())),
             preferred_element_type=F32,
@@ -574,14 +606,28 @@
             across,
         )
 
-    ow_copies[0].wait()
-    for n in range(chunks):
-        psend[n * piece : (n + 1) * piece, :] = project(0, n)
-        exchange(n).start()
-    ow_copies[1].wait()
-    for n in range(chunks):
-        span = slice(n * piece, (n + 1) * piece)
-        zbuf[place, span, :] = project(1, n)
+    for copy in ow_copies:
+        copy.wait()
+
+    def offer(index, carry):
+        far = index < own_parts
+        psend[part(index), :] = project(
+            jnp.where(far, 0, 1), jnp.where(far, index, index - early)
+        )
+        exchange(index).start()
+        return carry
+
+    lax.fori_loop(0, parts, offer, 0)
+
+    def keep(index, carry):
+        zbuf[place, part(index), :] = project(1, index)
+        return carry
+
+    lax.fori_loop(0, late, keep, 0)
+    zbuf[place, late * piece : half, :] = psend[half:, :]
+    zbuf[place, half:, :] = psend[late * piece : half, :]
+    for copy in res_copies:
+        copy.wait()
 
     def line_copy(owner, index, up):
         to = jnp.where(up == 1, place + 1, place - 1)
@@ -593,99 +639,74 @@
     def has_next(up):
         return jnp.where(up == 1, place + 1 < length, place > 0)
 
-    for copy in w_copies:
-        copy.wait()
-
-    def unpair(step, carry):
-        at = pl.ds(pl.multiple_of(step * 32, 32), 32)
-        pair = jnp.swapaxes(paired[at], 0, 1)
-        w[at, :width] = pair[0]
-        w[at, width:] = pair[1]
-        return carry
-
-    lax.fori_loop(0, w.shape[0] // 32, unpair, 0)
-
-    for n in range(chunks):
-        span = slice(n * piece, (n + 1) * piece)
-        exchange(n).wait_recv()
-        total = zbuf[place, span, :].astype(F32) + precv[span, :].astype(F32)
-        zbuf[place, span, :] = (res_ref[span, :].astype(F32) + total).astype(BF16)
+    def reduce(index):
+        exchange(index).wait_recv()
+        total = zbuf[place, part(index), :].astype(F32) + precv[part(index), :].astype(F32)
+        zbuf[place, part(index), :] = (res_ref[part(index), :].astype(F32) + total).astype(BF16)
         for up in range(2):
 
             @pl.when(has_next(up))
-            def _(n=n, up=up):
-                line_copy(place, n, up).start()
-
-    hid_copy = pltpu.make_async_copy(zbuf.at[place], hid_hbm, hid_sem)
-    hid_copy.start()
+            def _(up=up):
+                line_copy(place, index, up).start()
 
     for j in range(1, length):
         meta_landed(j).wait_recv()
 
     slots = lax.broadcasted_iota(jnp.int32, (cap, tokens), 0).astype(F32)
 
-    def y_copy(owner):
+    def y_copy(owner, index):
         return remote(
-            ysend.at[owner], rows.at[owner, 1], ysend_sem.at[owner], yrecv_sem.at[owner], partner
-        )
-
-    def x_copy(owner, which):
+            ysend.at[owner, index],
+            rows.at[owner, index, 1],
+            ysend_sem.at[owner, index],
+            yrecv_sem.at[owner, index],
+            partner,
+        )
+
+    def x_copy(owner, index, which):
         return remote(
-            rows.at[owner, which],
-            cross.at[owner, which],
-            xsend_sem.at[owner, which],
-            xrecv_sem.at[owner, which],
+            rows.at[owner, index, which],
+            cross.at[owner, index, which],
+            xsend_sem.at[owner, index, which],
+            xrecv_sem.at[owner, index, which],
             across,
         )
 
-    def pick(owner):
+    def pick(owner, index):
         def picks(expert):
             wanted = meta[owner, pl.ds(expert, 1), :]
             return jnp.where(slots == wanted, 1.0, 0.0)
 
         both = jnp.concatenate([picks(place * 2 + 1 - side), picks(me)], 0).astype(BF16)
         found = lax.dot_general(
-            both, zbuf[owner], (((1,), (1,)), ((), ())), preferred_element_type=F32
-        )
-        ysend[owner] = found[:cap].astype(BF16)
-        y_copy(owner).start()
-        rows[owner, 0] = found[cap:].astype(BF16)
-        x_copy(owner, 0).start()
-
-    def scaled(buffer, owner, n):
-        raw = buffer[owner].astype(F32).reshape(2 * cap, half)
+            both,
+            zbuf[owner, part(index), :],
+            (((1,), (1,)), ((), ())),
+            preferred_element_type=F32,
+        )
+        ysend[owner, index] = found[:cap].astype(BF16)
+        y_copy(owner, index).start()
+        rows[owner, index, 0] = found[cap:].astype(BF16)
+
+        @pl.when(index < late)
+        def _():
+            x_copy(owner, index, 0).start()
+
+    def gather(buffer, owner, index, at, fresh):
+        raw = buffer[owner, index].astype(F32).reshape(2 * cap, piece)
         squares = jnp.sum(raw * raw, axis=1, keepdims=True)
-        return squares, (raw * gains[n : n + 1, :]).astype(BF16)
-
-    def first(owner):
-        squares, left = scaled(rows, owner, 0)
-        sums[owner] = jnp.broadcast_to(squares, (2 * cap, sums.shape[2]))
+        left = (raw * gains[pl.ds(at, 1), :]).astype(BF16)
+        sums[owner] = jnp.where(fresh, 0.0, sums[owner]) + squares
         for low in (0, width):
-            acc[owner, :, low : low + width] = jnp.dot(
-                left, w[:half, low : low + width], preferred_element_type=F32
+            product = jnp.dot(
+                left, w[part(at), low : low + width], preferred_element_type=F32
             )
+            held = acc[owner, :, low : low + width]
+            acc[owner, :, low : low + width] = jnp.where(fresh, 0.0, held) + product
 
     def result(owner, which):
         source = owner * 2 + jnp.where(which == 0, side, 1 - side)
         return pltpu.make_async_copy(out.at[owner, which], act_hbm.at[source], out_sem.at[owner, which])
-
-    def second(owner):
-        squares, right = scaled(cross, owner, 1)
-        squares = squares + sums[owner][:, :1]
-        inverse_rms = lax.rsqrt(squares / (2 * half) + 1e-05)
-
-        def product(low):
-            return (
-                acc[owner, :, low : low + width]
-                + jnp.dot(right, w[half:, low : low + width], preferred_element_type=F32)
-            ) * inverse_rms
-
-        gate = product(0)
-        up = product(width)
-        active = gate * jax.nn.sigmoid(1.702 * gate) * (up + 1.0)
-        out[owner] = active.reshape(2, cap, width).astype(BF16)
-        for which in range(2):
-            result(owner, which).start()
 
     def owner_of(step, up):
         return jnp.where(up == 1, place + step, place - step)
@@ -704,66 +725,155 @@
 
         lax.fori_loop(0, 2, one, 0)
 
-    def arrive(owner, up):
-        @pl.when(owner != place)
+    def meet(owner, index):
+        y_copy(owner, index).wait_recv()
+
+        @pl.when(index < late)
         def _():
-            for n in range(chunks):
-                line_copy(owner, n, 1 - up).wait_recv()
+            x_copy(owner, index, 1).start()
+
+        gather(rows, owner, index, index, index == 0)
+
+    def finish(owner):
+        def add(index, carry):
+            for which in range(2):
+                x_copy(owner, index, which).wait_recv()
+            gather(cross, owner, index, parts + index, False)
+            return carry
+
+        lax.fori_loop(0, late, add, 0)
+        inverse_rms = lax.rsqrt(sums[owner][:, :1] / (2 * half) + 1e-05)
+        gate = acc[owner, :, :width] * inverse_rms
+        up = acc[owner, :, width:] * inverse_rms
+        active = gate * jax.nn.sigmoid(1.702 * gate) * (up + 1.0)
+        out[owner] = active.reshape(2, cap, width).astype(BF16)
+        for which in range(2):
+            result(owner, which).start()
+
+    hid_copy = pltpu.make_async_copy(zbuf.at[place, own_spot], hid_hbm, hid_sem)
+
+    turns = length * parts + 2
+
+    def advance(turn, carry):
+        step, index = turn // parts, lax.rem(turn, parts)
+
+        @pl.when(step == 0)
+        def _():
+            reduce(index)
+
+        @pl.when((step > 0) & (step < length))
+        def _():
+            def arrive(owner, up):
+                line_copy(owner, index, 1 - up).wait_recv()
 
                 @pl.when(has_next(1 - up))
-                def _(n=n):
-                    line_copy(owner, n, 1 - up).start()
-
-    def meet(owner, up):
-        y_copy(owner).wait_recv()
-        x_copy(owner, 1).start()
-        first(owner)
-
-    def finish(owner, up):
-        for which in range(2):
-            x_copy(owner, which).wait_recv()
-        second(owner)
-
-    def advance(step, carry):
-        each(step, arrive)
-        each(step, lambda owner, up: pick(owner))
-
-        @pl.when(step > 0)
+                def _():
+                    line_copy(owner, index, 1 - up).start()
+
+            each(step, arrive)
+
+        each(step, lambda owner, up: pick(owner, index))
+
+        @pl.when(turn == parts)
         def _():
-            each(step - 1, finish)
-
-        each(step, meet)
+            hid_copy.start()
+
+        @pl.when(turn >= 2)
+        def _():
+            last = turn - 2
+            each(last // parts, lambda owner, up: meet(owner, lax.rem(last, parts)))
+
+        done = jnp.where(step < length, index == parts - 1, turn == turns - 1)
+
+        @pl.when((step > 0) & done)
+        def _():
+            each(jnp.minimum(step, length) - 1, lambda owner, up: finish(owner))
+
         return carry
 
-    lax.fori_loop(0, length + 1, advance, 0)
+    lax.fori_loop(0, turns, advance, 0)
 
     def drain(owner, carry):
-        y_copy(owner).wait_send()
-        for which in range(2):
-            x_copy(owner, which).wait_send()
-            result(owner, which).wait()
-        for n in range(chunks):
+        def settle(index, carry):
+            y_copy(owner, index).wait_send()
             for up in range(2):
                 came = jnp.where(up == 1, owner <= place, owner >= place)
 
                 @pl.when(has_next(up) & came)
-                def _(n=n, up=up):
-                    line_copy(owner, n, up).wait_send()
-
+                def _(up=up):
+                    line_copy(owner, index, up).wait_send()
+
+            @pl.when(index < late)
+            def _():
+                for which in range(2):
+                    x_copy(owner, index, which).wait_send()
+
+            return carry
+
+        lax.fori_loop(0, parts, settle, 0)
+        for which in range(2):
+            result(owner, which).wait()
         return carry
 
     lax.fori_loop(0, length, drain, 0)
     hid_copy.wait()
     for j in range(1, length):
         meta_copy(j).wait_send()
-    for n in range(chunks):
-        exchange(n).wait_send()
+
+    def settle_exchange(index, carry):
+        exchange(index).wait_send()
+        return carry
+
+    lax.fori_loop(0, parts, settle_exchange, 0)
     for j in range(1, reach + 1):
 
         @pl.when(block + j < blocks)
         def _(j=j):
             for copy in window_copies(j):
                 copy.wait_send()
+
+
+def place_kernel(hid_in, act_in, hid_out, act_out, hid, act, in_sem, out_sem):
+    pieces = act_in.shape[0]
+    parts = max(n for n in range(1, pieces + 1) if hid_in.shape[0] % (16 * n) == 0)
+    size = hid_in.shape[0] // parts
+    spots = [(hid_in, hid, hid_out, pl.ds(n * size, size)) for n in range(parts)]
+    spots += [(act_in, act, act_out, n) for n in range(pieces)]
+    loads = [
+        pltpu.make_async_copy(source.at[at], held.at[at], in_sem.at[n])
+        for n, (source, held, _, at) in enumerate(spots)
+    ]
+    stores = [
+        pltpu.make_async_copy(held.at[at], target.at[at], out_sem.at[n])
+        for n, (_, held, target, at) in enumerate(spots)
+    ]
+    for copy in loads:
+        copy.start()
+    for load, store in zip(loads, stores):
+        load.wait()
+        store.start()
+    for copy in stores:
+        copy.wait()
+
+
+def placed(hidden, active):
+    in_hbm = pl.BlockSpec(memory_space=pl.ANY)
+    pieces = active.shape[0]
+    return pl.pallas_call(
+        place_kernel,
+        out_shape=(
+            jax.ShapeDtypeStruct(hidden.shape, hidden.dtype),
+            jax.ShapeDtypeStruct(active.shape, active.dtype),
+        ),
+        in_specs=[in_hbm] * 2,
+        out_specs=(in_hbm, in_hbm),
+        scratch_shapes=[
+            pltpu.VMEM(hidden.shape, hidden.dtype),
+            pltpu.VMEM(active.shape, active.dtype),
+            pltpu.SemaphoreType.DMA((2 * pieces,)),
+            pltpu.SemaphoreType.DMA((2 * pieces,)),
+        ],
+    )(hidden, active)
 
 
 def along_line(
@@ -774,12 +884,16 @@
     half = width_all // 2
     length = count // 2
     width = expert_weight.shape[3]
-    chunks = max(n for n in range(1, 4) if half % (16 * n) == 0)
+    pieces = max(n for n in range(1, 3 + 1) if half % (16 * n) == 0)
+    early = min(1, pieces - 1)
+    late = pieces - early
+    parts = pieces + early
+    piece = half // pieces
     in_vmem = pl.BlockSpec(memory_space=pltpu.VMEM)
     in_hbm = pl.BlockSpec(memory_space=pl.ANY)
     dma = pltpu.SemaphoreType.DMA
     return pl.pallas_call(
-        functools.partial(line_kernel, count, cap, reach, chunks),
+        functools.partial(line_kernel, count, cap, reach, late, early),
         out_shape=(
             jax.ShapeDtypeStruct((half, tokens), BF16),
             jax.ShapeDtypeStruct((count, cap, width), BF16),
@@ -790,37 +904,37 @@
             pltpu.VMEM(queries.shape, BF16),
             pltpu.VMEM(((reach + 1) * tokens, keys.shape[1]), BF16),
             pltpu.VMEM(((reach + 1) * tokens, values.shape[1]), BF16),
-            pltpu.VMEM((half, tokens), BF16),
+            pltpu.VMEM((parts * piece, tokens), BF16),
             pltpu.VMEM(queries.shape, BF16),
             pltpu.VMEM((2, half, out_weight.shape[0]), BF16),
             pltpu.VMEM((width_all, 2, width), BF16),
             pltpu.VMEM((width_all, 2 * width), BF16),
-            pltpu.VMEM((2, half), F32),
-            pltpu.VMEM((half, tokens), BF16),
-            pltpu.VMEM((half, tokens), BF16),
+            pltpu.VMEM((2 * pieces, piece), F32),
+            pltpu.VMEM((parts * piece, tokens), BF16),
+            pltpu.VMEM((parts * piece, tokens), BF16),
             pltpu.VMEM((length, count, tokens), F32),
-            pltpu.VMEM((length, half, tokens), BF16),
-            pltpu.VMEM((length, cap, half), BF16),
-            pltpu.VMEM((length, 2, cap, half), BF16),
-            pltpu.VMEM((length, 2, cap, half), BF16),
+            pltpu.VMEM((length, parts * piece, tokens), BF16),
+            pltpu.VMEM((length, parts, cap, piece), BF16),
+            pltpu.VMEM((length, parts, 2, cap, piece), BF16),
+            pltpu.VMEM((length, late, 2, cap, piece), BF16),
             pltpu.VMEM((length, 2 * cap, 2 * width), F32),
             pltpu.VMEM((length, 2 * cap, 128), F32),
             pltpu.VMEM((length, 2, cap, width), BF16),
-            dma((4,)),
+            dma((5,)),
             dma((2, reach)),
             dma((2, reach)),
             dma((2,)),
-            dma((2,)),
-            dma((chunks,)),
-            dma((chunks,)),
+            dma((3,)),
+            dma((parts,)),
+            dma((parts,)),
             dma((length - 1,)),
             dma((length,)),
-            dma((2, length, chunks)),
-            dma((length, chunks)),
-            dma((length,)),
-            dma((length,)),
-            dma((length, 2)),
-            dma((length, 2)),
+            dma((2, length, parts)),
+            dma((length, parts)),
+            dma((length, parts)),
+            dma((length, parts)),
+            dma((length, late, 2)),
+            dma((length, late, 2)),
             dma,
             dma((length, 2)),
         ],
@@ -833,7 +947,7 @@
         values,
         residual.T,
         routes.T,
-        norm_gain.reshape(1, width_all),
+        norm_gain,
         out_weight.T,
         expert_weight[0],
     )
@@ -864,6 +978,7 @@
             out_weight,
             expert_weight,
         )
+        hidden, active = placed(hidden, active)
         return (hidden.T, active.reshape(1, 1, count * cap, hidden_width))
     in_vmem = pl.BlockSpec(memory_space=pltpu.VMEM)
     in_hbm = pl.BlockSpec(memory_space=pl.ANY)

time: 70.8 us -> 60.6 us (0.86)
  local copies, waits for them, and re-layouts: 5.2 us -> 0 us
  Pallas kernels: 64.6 us -> 59.7 us
    pallas_call x1 -> x2, Pallas kernels: 64.6 us -> 59.7 us  [the longest x1 57.4 us: along_line(): pl.pallas_call(functools.partial(line_kernel, count, cap, reach, late, ea...]
    unnamed x2 -> x0, local copies, waits for them, and re-layouts: 3.88 us -> none
    reshape x1 -> x0, local copies, waits for them, and re-layouts: 1.31 us -> none  [along_line(): norm_gain.reshape(1, width_all)]
where the time goes in v3:
time: 60.6 us; the launch traced here: 60.4 us
  Pallas kernels  59.7 us (99%)
  between operations  0.64 us (1%)
    pallas_call x1, Pallas kernels, along_line(): pl.pallas_call(functools.partial(line_kernel, count, cap, reach, late, ea...  57.4 us
    pallas_call x1, Pallas kernels, placed(): pl.pallas_call(place_kernel, out_shape=(jax.ShapeDtypeStruct(hidden.shape...  2.31 us

profile of v3, /device:TPU:0, one launch (start us, length us, event | category | flops | bytes accessed | tf_op | source)
XLA Modules:
  0.0 60.4 jit_solution(6901276591876156890)
XLA Ops:
  0.6 57.4 %shard_map.95 = (bf16[1440,128]{1,0:T(8,128)(2,1)}, bf16[8,72,768]{2,1,0:T(8,128)(2,1)}) custom-call(bf16[128,1024]{1,0:T(8,128)(2,1)} %q_hbm.1, bf16[128,128]{1,0:T(8,128)(2,1)} %k_hbm.1, bf16[128,128]{1,0:T(8,128)(2,1)} %v_hbm.1, bf16[2880,128]{1,0:T(8,128)(2,1)} %bitcast.8, s32[4,128]{1,0:T(4,128)} %bitcast.9, f32[2880]{0:T(1024)} %gain_ref.1, ...), custom_call_target="tpu_custom_call" | custom-call | tf_op jit(solution)/shard_map/pallas_call | solution.py:895
  58.0 2.3 %shard_map.96 = (bf16[1440,128]{1,0:T(8,128)(2,1)}, bf16[8,72,768]{2,1,0:T(8,128)(2,1)}) custom-call(bf16[1440,128]{1,0:T(8,128)(2,1)} %get-tuple-element.6.hid_in, bf16[8,72,768]{2,1,0:T(8,128)(2,1)} %get-tuple-element.7.act_in), custom_call_target="tpu_custom_call" | custom-call | tf_op jit(solution)/shard_map/pallas_call | solution.py:862

commit v4 on v3

--- a/solution.py
+++ b/solution.py
@@ -375,7 +375,6 @@
     cap,
     reach,
     late,
-    early,
     q_hbm,
     k_hbm,
     v_hbm,
@@ -431,9 +430,9 @@
     side = lax.rem(me, 2)
     half, tokens = hid_hbm.shape
     width = act_hbm.shape[2]
-    own_parts = late + early
-    parts = own_parts + early
-    piece = half // own_parts
+    parts = late + 2
+    piece = rows.shape[4]
+    rest = half - late * piece
     groups = lax.axis_size("grp")
     block = me * groups + lax.axis_index("grp")
     blocks = count * groups
@@ -448,43 +447,55 @@
     across = {"head": other}
 
     barrier = pltpu.get_barrier_semaphore()
-    peers = [on_line(lax.rem(place + j, length)) for j in range(1, length)]
-    peers += [partner, across]
+    expected = 2
+    for peer in (partner, across):
+        pl.semaphore_signal(barrier, inc=1, device_id=peer, device_id_type=MESH)
+
+    def greet(there, peer):
+        @pl.when(there)
+        def _():
+            pl.semaphore_signal(barrier, inc=1, device_id=peer, device_id_type=MESH)
+
+        return jnp.where(there, 1, 0)
+
+    expected = expected + greet(place > 0, on_line(place - 1))
+    expected = expected + greet(place + 1 < length, on_line(place + 1))
     for j in range(1, reach + 1):
-        peers += [at_block(lax.rem(block + j, blocks)), at_block(lax.rem(block + blocks - j, blocks))]
-    for peer in peers:
-        pl.semaphore_signal(barrier, inc=1, device_id=peer, device_id_type=MESH)
-
-    def span(which, start, stop):
-        return pl.ds(pl.multiple_of(which * half + start * piece, 16), (stop - start) * piece)
-
+        expected = expected + greet(block + j < blocks, at_block(block + j))
+        expected = expected + greet(block >= j, at_block(block - j))
+
+    def span(which, start, size):
+        return pl.ds(pl.multiple_of(which * half + start, 16), size)
+
+    late_size = late * piece
+    far_start = (late + 1) * piece
     mine = pl.ds(reach * tokens, tokens)
     own_spot = pl.ds(0, half)
-    early_spot = pl.ds(half, early * piece)
-    late_spot = pl.ds(parts * piece, late * piece)
+    early_spot = pl.ds(far_start, rest)
+    late_spot = pl.ds(parts * piece, late_size)
     local = [
         pltpu.make_async_copy(k_hbm, kbuf.at[mine], in_sem.at[0]),
         pltpu.make_async_copy(v_hbm, vbuf.at[mine], in_sem.at[1]),
         pltpu.make_async_copy(q_hbm, q_ref, in_sem.at[2]),
     ]
     res_copies = [
-        pltpu.make_async_copy(res_hbm.at[span(head, 0, own_parts)], res_ref.at[own_spot], in_sem.at[3]),
+        pltpu.make_async_copy(res_hbm.at[span(head, 0, half)], res_ref.at[own_spot], in_sem.at[3]),
         pltpu.make_async_copy(
-            res_hbm.at[span(other, late, own_parts)], res_ref.at[early_spot], in_sem.at[4]
+            res_hbm.at[span(other, late_size, rest)], res_ref.at[early_spot], in_sem.at[4]
         ),
     ]
     w_copies = [
-        pltpu.make_async_copy(w_hbm.at[span(which, low, high)], paired.at[spot], w_sem.at[n])
-        for n, (which, low, high, spot) in enumerate(
+        pltpu.make_async_copy(w_hbm.at[span(which, start, size)], paired.at[spot], w_sem.at[n])
+        for n, (which, start, size, spot) in enumerate(
             (
-                (head, 0, own_parts, own_spot),
-                (other, late, own_parts, early_spot),
-                (other, 0, late, late_spot),
+                (head, 0, half, own_spot),
+                (other, late_size, rest, early_spot),
+                (other, 0, late_size, late_spot),
             )
         )
     ]
     ow_copies = [
-        pltpu.make_async_copy(ow_hbm.at[span(which, 0, own_parts)], ow.at[n], ow_sem.at[n])
+        pltpu.make_async_copy(ow_hbm.at[span(which, 0, half)], ow.at[n], ow_sem.at[n])
         for n, which in enumerate((other, head))
     ]
     for copy in local + w_copies + ow_copies + res_copies:
@@ -502,7 +513,7 @@
 
     def window_copies(j):
         rows_at = pl.ds((reach - j) * tokens, tokens)
-        target = at_block(lax.rem(block + j, blocks))
+        target = at_block(block + j)
         return [
             remote(source, buffer.at[rows_at], ksend_sem.at[n, j - 1], krecv_sem.at[n, j - 1], target)
             for n, (source, buffer) in enumerate(((k_hbm, kbuf), (v_hbm, vbuf)))
@@ -522,14 +533,19 @@
     meta[place] = jnp.where(hits > 0.5, before, -1.0)
 
     gain = gain_ref[...].reshape(1, 2 * half)
-    order = [(0, n) for n in range(own_parts)]
-    order += [(1, n) for n in range(late, own_parts)] + [(1, n) for n in range(late)]
+    gains[...] = jnp.zeros(gains.shape, F32)
+    order = [(0, n) for n in range(late + 1)] + [(1, late)] + [(1, n) for n in range(late)]
     for n, (far, index) in enumerate(order):
-        left = gain[:, index * piece : (index + 1) * piece]
-        right = gain[:, half + index * piece : half + (index + 1) * piece]
-        gains[n : n + 1, :] = jnp.where(head == far, left, right)
-
-    pl.semaphore_wait(barrier, len(peers))
+        size = piece if index < late else rest
+        left = gain[:, index * piece : index * piece + size]
+        right = gain[:, half + index * piece : half + index * piece + size]
+        gains[n : n + 1, :size] = jnp.where(head == far, left, right)
+    if rest < piece:
+        blank = piece - rest
+        for start in (half, far_start + rest):
+            zbuf[:, start : start + blank, :] = jnp.zeros((length, blank, tokens), BF16)
+
+    pl.semaphore_wait(barrier, expected)
     for j in range(1, reach + 1):
 
         @pl.when(block + j < blocks)
@@ -537,23 +553,19 @@
             for copy in window_copies(j):
                 copy.start()
 
-    def meta_copy(j):
-        return remote(
-            meta.at[place],
-            meta.at[place],
-            msend_sem.at[j - 1],
-            mrecv_sem.at[place],
-            on_line(lax.rem(place + j, length)),
-        )
-
-    def meta_landed(j):
-        source = lax.rem(place + length - j, length)
-        return remote(
-            meta.at[source], meta.at[source], msend_sem.at[j - 1], mrecv_sem.at[source], across
-        )
-
-    for j in range(1, length):
-        meta_copy(j).start()
+    def meta_copy(owner, up):
+        to = jnp.where(up == 1, place + 1, place - 1)
+        spot = meta.at[owner]
+        return remote(spot, spot, msend_sem.at[up, owner], mrecv_sem.at[owner], on_line(to))
+
+    def has_next(up):
+        return jnp.where(up == 1, place + 1 < length, place > 0)
+
+    for up in range(2):
+
+        @pl.when(has_next(up))
+        def _(up=up):
+            meta_copy(place, up).start()
 
     for copy in w_copies:
         copy.wait()
@@ -566,6 +578,9 @@
         return carry
 
     lax.fori_loop(0, w.shape[0] // 32, unpair, 0)
+    if rest < piece:
+        for start in (half, far_start + rest):
+            w[start : start + blank, :] = jnp.zeros((blank, 2 * width), BF16)
 
     for j in range(1, reach + 1):
 
@@ -586,22 +601,31 @@
 
     attend(block, reach, q_ref, kbuf, vbuf, att_ref)
 
-    def part(index):
-        return pl.ds(pl.multiple_of(index * piece, 16), piece)
-
-    def project(slot, index):
+    def part(index, size=piece):
+        return pl.ds(pl.multiple_of(index * piece, 16), size)
+
+    def sized(index, action):
+        @pl.when(index < late)
+        def _():
+            action(piece)
+
+        @pl.when(index >= late)
+        def _():
+            action(rest)
+
+    def project(slot, index, size):
         return lax.dot_general(
-            ow[slot, part(index), :],
+            ow[slot, part(index, size), :],
             att_ref[...],
             (((1,), (1,)), ((), ())),
             preferred_element_type=F32,
         ).astype(BF16)
 
-    def exchange(index):
+    def exchange(index, size):
         return remote(
-            psend.at[part(index)],
-            precv.at[part(index)],
-            psend_sem.at[index],
+            psend.at[part(index, size)],
+            precv.at[part(index, size)],
+            psend_sem,
             precv_sem.at[index],
             across,
         )
@@ -610,47 +634,42 @@
         copy.wait()
 
     def offer(index, carry):
-        far = index < own_parts
-        psend[part(index), :] = project(
-            jnp.where(far, 0, 1), jnp.where(far, index, index - early)
-        )
-        exchange(index).start()
+        psend[part(index), :] = project(0, index, piece)
+        exchange(index, piece).start()
         return carry
 
-    lax.fori_loop(0, parts, offer, 0)
+    lax.fori_loop(0, late, offer, 0)
+    for n in range(2):
+        psend[part(late + n, rest), :] = project(n, late, rest)
+        exchange(late + n, rest).start()
 
     def keep(index, carry):
-        zbuf[place, part(index), :] = project(1, index)
+        zbuf[place, part(index), :] = project(1, index, piece)
         return carry
 
     lax.fori_loop(0, late, keep, 0)
-    zbuf[place, late * piece : half, :] = psend[half:, :]
-    zbuf[place, half:, :] = psend[late * piece : half, :]
+    zbuf[place, part(late, rest), :] = psend[part(late + 1, rest), :]
+    zbuf[place, part(late + 1, rest), :] = psend[part(late, rest), :]
     for copy in res_copies:
         copy.wait()
 
-    def line_copy(owner, index, up):
+    def line_copy(owner, index, up, size):
         to = jnp.where(up == 1, place + 1, place - 1)
-        spot = zbuf.at[owner, part(index)]
+        spot = zbuf.at[owner, part(index, size)]
         return remote(
-            spot, spot, zsend_sem.at[up, owner, index], zrecv_sem.at[owner, index], on_line(to)
-        )
-
-    def has_next(up):
-        return jnp.where(up == 1, place + 1 < length, place > 0)
-
-    def reduce(index):
-        exchange(index).wait_recv()
-        total = zbuf[place, part(index), :].astype(F32) + precv[part(index), :].astype(F32)
-        zbuf[place, part(index), :] = (res_ref[part(index), :].astype(F32) + total).astype(BF16)
+            spot, spot, zsend_sem.at[up, owner], zrecv_sem.at[owner, index], on_line(to)
+        )
+
+    def reduce(index, size):
+        at = part(index, size)
+        exchange(index, size).wait_recv()
+        total = zbuf[place, at, :].astype(F32) + precv[at, :].astype(F32)
+        zbuf[place, at, :] = (res_ref[at, :].astype(F32) + total).astype(BF16)
         for up in range(2):
 
             @pl.when(has_next(up))
             def _(up=up):
-                line_copy(place, index, up).start()
-
-    for j in range(1, length):
-        meta_landed(j).wait_recv()
+                line_copy(place, index, up, size).start()
 
     slots = lax.broadcasted_iota(jnp.int32, (cap, tokens), 0).astype(F32)
 
@@ -658,7 +677,7 @@
         return remote(
             ysend.at[owner, index],
             rows.at[owner, index, 1],
-            ysend_sem.at[owner, index],
+            ysend_sem,
             yrecv_sem.at[owner, index],
             partner,
         )
@@ -667,7 +686,7 @@
         return remote(
             rows.at[owner, index, which],
             cross.at[owner, index, which],
-            xsend_sem.at[owner, index, which],
+            xsend_sem,
             xrecv_sem.at[owner, index, which],
             across,
         )
@@ -706,7 +725,7 @@
 
     def result(owner, which):
         source = owner * 2 + jnp.where(which == 0, side, 1 - side)
-        return pltpu.make_async_copy(out.at[owner, which], act_hbm.at[source], out_sem.at[owner, which])
+        return pltpu.make_async_copy(out.at[owner, which], act_hbm.at[source], out_sem)
 
     def owner_of(step, up):
         return jnp.where(up == 1, place + step, place - step)
@@ -734,7 +753,7 @@
 
         gather(rows, owner, index, index, index == 0)
 
-    def finish(owner):
+    def take(owner):
         def add(index, carry):
             for which in range(2):
                 x_copy(owner, index, which).wait_recv()
@@ -742,6 +761,8 @@
             return carry
 
         lax.fori_loop(0, late, add, 0)
+
+    def close(owner):
         inverse_rms = lax.rsqrt(sums[owner][:, :1] / (2 * half) + 1e-05)
         gate = acc[owner, :, :width] * inverse_rms
         up = acc[owner, :, width:] * inverse_rms
@@ -752,79 +773,94 @@
 
     hid_copy = pltpu.make_async_copy(zbuf.at[place, own_spot], hid_hbm, hid_sem)
 
-    turns = length * parts + 2
-
-    def advance(turn, carry):
-        step, index = turn // parts, lax.rem(turn, parts)
+    lag = 2
+
+    def turn(step, index):
+        late_turn = index < lag
+        met_step = jnp.where(late_turn, step - 1, step)
+        met_index = jnp.where(late_turn, index + parts - lag, index - lag)
+        ending = jnp.where(step < length, parts - 1, lag - 1)
+        closing = (step > 0) & (index == ending)
 
         @pl.when(step == 0)
         def _():
-            reduce(index)
-
-        @pl.when((step > 0) & (step < length))
-        def _():
-            def arrive(owner, up):
-                line_copy(owner, index, 1 - up).wait_recv()
-
-                @pl.when(has_next(1 - up))
+            sized(index, lambda size: reduce(index, size))
+
+        def collect(owner, up):
+            @pl.when(step > 0)
+            def _():
+                @pl.when(index == 0)
                 def _():
-                    line_copy(owner, index, 1 - up).start()
-
-            each(step, arrive)
-
-        each(step, lambda owner, up: pick(owner, index))
-
-        @pl.when(turn == parts)
+                    meta_copy(owner, 1 - up).wait_recv()
+
+                    @pl.when(has_next(1 - up))
+                    def _():
+                        meta_copy(owner, 1 - up).start()
+
+                def pass_on(size):
+                    line_copy(owner, index, 1 - up, size).wait_recv()
+
+                    @pl.when(has_next(1 - up))
+                    def _():
+                        line_copy(owner, index, 1 - up, size).start()
+
+                sized(index, pass_on)
+
+            pick(owner, index)
+
+        each(step, collect)
+
+        @pl.when((step == 1) & (index == 0))
         def _():
             hid_copy.start()
 
-        @pl.when(turn >= 2)
+        @pl.when(closing)
         def _():
-            last = turn - 2
-            each(last // parts, lambda owner, up: meet(owner, lax.rem(last, parts)))
-
-        done = jnp.where(step < length, index == parts - 1, turn == turns - 1)
-
-        @pl.when((step > 0) & done)
+            each(step - 1, lambda owner, up: take(owner))
+
+        @pl.when(met_step >= 0)
         def _():
-            each(jnp.minimum(step, length) - 1, lambda owner, up: finish(owner))
-
+            each(met_step, lambda owner, up: meet(owner, met_index))
+
+        @pl.when(closing)
+        def _():
+            each(step - 1, lambda owner, up: close(owner))
+
+    def advance(step, carry):
+        def one(index, carry):
+            turn(step, index)
+            return carry
+
+        lax.fori_loop(0, jnp.where(step < length, parts, lag), one, 0)
         return carry
 
-    lax.fori_loop(0, turns, advance, 0)
+    lax.fori_loop(0, length + 1, advance, 0)
+
+    y_whole = remote(ysend, ysend, ysend_sem, yrecv_sem.at[0, 0], partner)
+    x_whole = remote(cross, cross, xsend_sem, xrecv_sem.at[0, 0, 0], across)
+    y_whole.wait_send()
+    x_whole.wait_send()
 
     def drain(owner, carry):
-        def settle(index, carry):
-            y_copy(owner, index).wait_send()
-            for up in range(2):
-                came = jnp.where(up == 1, owner <= place, owner >= place)
-
-                @pl.when(has_next(up) & came)
-                def _(up=up):
-                    line_copy(owner, index, up).wait_send()
-
-            @pl.when(index < late)
-            def _():
-                for which in range(2):
-                    x_copy(owner, index, which).wait_send()
-
-            return carry
-
-        lax.fori_loop(0, parts, settle, 0)
-        for which in range(2):
-            result(owner, which).wait()
+        for up in range(2):
+            came = jnp.where(up == 1, owner <= place, owner >= place)
+
+            @pl.when(has_next(up) & came)
+            def _(up=up):
+                meta_copy(owner, up).wait_send()
+                sent = zbuf.at[owner, pl.ds(0, half + rest)]
+                remote(
+                    sent, sent, zsend_sem.at[up, owner], zrecv_sem.at[owner, 0], across
+                ).wait_send()
+
         return carry
 
     lax.fori_loop(0, length, drain, 0)
+    pltpu.make_async_copy(out, out, out_sem).wait()
     hid_copy.wait()
-    for j in range(1, length):
-        meta_copy(j).wait_send()
-
-    def settle_exchange(index, carry):
-        exchange(index).wait_send()
-        return carry
-
-    lax.fori_loop(0, parts, settle_exchange, 0)
+    sent = psend.at[pl.ds(0, half + rest)]
+    remote(sent, sent, psend_sem, precv_sem.at[0], across).wait_send()
+
     for j in range(1, reach + 1):
 
         @pl.when(block + j < blocks)
@@ -884,16 +920,15 @@
     half = width_all // 2
     length = count // 2
     width = expert_weight.shape[3]
-    pieces = max(n for n in range(1, 3 + 1) if half % (16 * n) == 0)
-    early = min(1, pieces - 1)
-    late = pieces - early
-    parts = pieces + early
-    piece = half // pieces
+    piece = min(384, half // 32 * 16)
+    late = (half - 16) // piece
+    parts = late + 2
+    total = parts + late
     in_vmem = pl.BlockSpec(memory_space=pltpu.VMEM)
     in_hbm = pl.BlockSpec(memory_space=pl.ANY)
     dma = pltpu.SemaphoreType.DMA
     return pl.pallas_call(
-        functools.partial(line_kernel, count, cap, reach, late, early),
+        functools.partial(line_kernel, count, cap, reach, late),
         out_shape=(
             jax.ShapeDtypeStruct((half, tokens), BF16),
             jax.ShapeDtypeStruct((count, cap, width), BF16),
@@ -907,9 +942,9 @@
             pltpu.VMEM((parts * piece, tokens), BF16),
             pltpu.VMEM(queries.shape, BF16),
             pltpu.VMEM((2, half, out_weight.shape[0]), BF16),
-            pltpu.VMEM((width_all, 2, width), BF16),
-            pltpu.VMEM((width_all, 2 * width), BF16),
-            pltpu.VMEM((2 * pieces, piece), F32),
+            pltpu.VMEM((total * piece, 2, width), BF16),
+            pltpu.VMEM((total * piece, 2 * width), BF16),
+            pltpu.VMEM((total, piece), F32),
             pltpu.VMEM((parts * piece, tokens), BF16),
             pltpu.VMEM((parts * piece, tokens), BF16),
             pltpu.VMEM((length, count, tokens), F32),
@@ -925,18 +960,18 @@
             dma((2, reach)),
             dma((2,)),
             dma((3,)),
+            dma,
             dma((parts,)),
-            dma((parts,)),
-            dma((length - 1,)),
+            dma((2, length)),
             dma((length,)),
-            dma((2, length, parts)),
+            dma((2, length)),
             dma((length, parts)),
+            dma,
             dma((length, parts)),
-            dma((length, parts)),
-            dma((length, late, 2)),
+            dma,
             dma((length, late, 2)),
             dma,
-            dma((length, 2)),
+            dma,
         ],
         compiler_params=pltpu.CompilerParams(
             collective_id=1, has_side_effects=True, vmem_limit_bytes=60 * 1024 * 1024

time: 60.6 us -> 58.5 us (0.965)
  Pallas kernels: 59.7 us -> 57.7 us
    pallas_call x1, Pallas kernels: 57.4 us -> 55.3 us  [along_line(): pl.pallas_call(functools.partial(line_kernel, count, cap, reach, late), o...]
where the time goes in v4:
time: 58.5 us; the launch traced here: 58.3 us
  Pallas kernels  57.7 us (99%)
  between operations  0.64 us (1%)
    pallas_call x1, Pallas kernels, along_line(): pl.pallas_call(functools.partial(line_kernel, count, cap, reach, late), o...  55.3 us
    pallas_call x1, Pallas kernels, placed(): pl.pallas_call(place_kernel, out_shape=(jax.ShapeDtypeStruct(hidden.shape...  2.31 us

profile of v4, /device:TPU:0, one launch (start us, length us, event | category | flops | bytes accessed | tf_op | source)
XLA Modules:
  0.0 58.3 jit_solution(2283079729024256146)
XLA Ops:
  0.6 55.3 %shard_map.95 = (bf16[1440,128]{1,0:T(8,128)(2,1)}, bf16[8,72,768]{2,1,0:T(8,128)(2,1)}) custom-call(bf16[128,1024]{1,0:T(8,128)(2,1)} %q_hbm.1, bf16[128,128]{1,0:T(8,128)(2,1)} %k_hbm.1, bf16[128,128]{1,0:T(8,128)(2,1)} %v_hbm.1, bf16[2880,128]{1,0:T(8,128)(2,1)} %bitcast.8, s32[4,128]{1,0:T(4,128)} %bitcast.9, f32[2880]{0:T(1024)} %gain_ref.1, ...), custom_call_target="tpu_custom_call" | custom-call | tf_op jit(solution)/shard_map/pallas_call | solution.py:930
  56.0 2.3 %shard_map.96 = (bf16[1440,128]{1,0:T(8,128)(2,1)}, bf16[8,72,768]{2,1,0:T(8,128)(2,1)}) custom-call(bf16[1440,128]{1,0:T(8,128)(2,1)} %get-tuple-element.6.hid_in, bf16[8,72,768]{2,1,0:T(8,128)(2,1)} %get-tuple-element.7.act_in), custom_call_target="tpu_custom_call" | custom-call | tf_op jit(solution)/shard_map/pallas_call | solution.py:898

commit v5 on v4

--- a/solution.py
+++ b/solution.py
@@ -9,6 +9,7 @@
 D = 2880
 HD = 64
 TOP = 4
+PIECE = 3 * 128
 
 
 MESH = pl.DeviceIdType.MESH
@@ -498,7 +499,7 @@
         pltpu.make_async_copy(ow_hbm.at[span(which, 0, half)], ow.at[n], ow_sem.at[n])
         for n, which in enumerate((other, head))
     ]
-    for copy in local + w_copies + ow_copies + res_copies:
+    for copy in local + ow_copies + res_copies + w_copies:
         copy.start()
 
     def remote(source, target, send, recv, device):
@@ -544,6 +545,7 @@
         blank = piece - rest
         for start in (half, far_start + rest):
             zbuf[:, start : start + blank, :] = jnp.zeros((length, blank, tokens), BF16)
+            paired[start : start + blank] = jnp.zeros((blank, 2, width), BF16)
 
     pl.semaphore_wait(barrier, expected)
     for j in range(1, reach + 1):
@@ -566,21 +568,6 @@
         @pl.when(has_next(up))
         def _(up=up):
             meta_copy(place, up).start()
-
-    for copy in w_copies:
-        copy.wait()
-
-    def unpair(step, carry):
-        at = pl.ds(pl.multiple_of(step * 32, 32), 32)
-        pair = jnp.swapaxes(paired[at], 0, 1)
-        w[at, :width] = pair[0]
-        w[at, width:] = pair[1]
-        return carry
-
-    lax.fori_loop(0, w.shape[0] // 32, unpair, 0)
-    if rest < piece:
-        for start in (half, far_start + rest):
-            w[start : start + blank, :] = jnp.zeros((blank, 2 * width), BF16)
 
     for j in range(1, reach + 1):
 
@@ -650,8 +637,19 @@
     lax.fori_loop(0, late, keep, 0)
     zbuf[place, part(late, rest), :] = psend[part(late + 1, rest), :]
     zbuf[place, part(late + 1, rest), :] = psend[part(late, rest), :]
-    for copy in res_copies:
+    for copy in res_copies + w_copies:
         copy.wait()
+
+    def unpair(index):
+        def one(step, carry):
+            at = pl.ds(pl.multiple_of(index * piece + step * 32, 32), 32)
+            pair = jnp.swapaxes(paired[at], 0, 1)
+            w[at, :width] = pair[0]
+            w[at, width:] = pair[1]
+            return carry
+
+        lax.fori_loop(0, piece // 32, one, 0)
+
 
     def line_copy(owner, index, up, size):
         to = jnp.where(up == 1, place + 1, place - 1)
@@ -810,6 +808,15 @@
 
         each(step, collect)
 
+        @pl.when(step == 0)
+        def _():
+            for n in range(2):
+                which = index * 2 + n
+
+                @pl.when(which < w.shape[0] // piece)
+                def _(which=which):
+                    unpair(which)
+
         @pl.when((step == 1) & (index == 0))
         def _():
             hid_copy.start()
@@ -870,11 +877,11 @@
 
 
 def place_kernel(hid_in, act_in, hid_out, act_out, hid, act, in_sem, out_sem):
-    pieces = act_in.shape[0]
-    parts = max(n for n in range(1, pieces + 1) if hid_in.shape[0] % (16 * n) == 0)
+    pieces = 4
+    parts = 2
     size = hid_in.shape[0] // parts
     spots = [(hid_in, hid, hid_out, pl.ds(n * size, size)) for n in range(parts)]
-    spots += [(act_in, act, act_out, n) for n in range(pieces)]
+    spots += [(act_in, act, act_out, pl.ds(n * (act_in.shape[0] // pieces), act_in.shape[0] // pieces)) for n in range(pieces)]
     loads = [
         pltpu.make_async_copy(source.at[at], held.at[at], in_sem.at[n])
         for n, (source, held, _, at) in enumerate(spots)
@@ -920,7 +927,7 @@
     half = width_all // 2
     length = count // 2
     width = expert_weight.shape[3]
-    piece = min(384, half // 32 * 16)
+    piece = PIECE
     late = (half - 16) // piece
     parts = late + 2
     total = parts + late
@@ -999,7 +1006,7 @@
     routed = tokens_here * TOP
     cap = min(tokens_here, routed // experts_all + max(1, routed // (8 * experts_all)))
     hidden_width = expert_weight.shape[3]
-    if heads_count == 2 and count % 2 == 0 and experts_all == count and 2 * cap >= tokens_here:
+    if heads_count == 2 and count % 2 == 0 and experts_all == count and 2 * cap >= tokens_here and half >= 2 * PIECE:
         hidden, active = along_line(
             count,
             cap,

time: 58.5 us -> 56.6 us (0.968)
  Pallas kernels: 57.7 us -> 55.7 us
    pallas_call x1, Pallas kernels: 55.3 us -> 53.4 us  [along_line(): pl.pallas_call(functools.partial(line_kernel, count, cap, reach, late), o...]
where the time goes in v5:
time: 56.6 us; the launch traced here: 56.4 us
  Pallas kernels  55.7 us (98%)
  between operations  0.64 us (1%)
    pallas_call x1, Pallas kernels, along_line(): pl.pallas_call(functools.partial(line_kernel, count, cap, reach, late), o...  53.4 us
    pallas_call x1, Pallas kernels, placed(): pl.pallas_call(place_kernel, out_shape=(jax.ShapeDtypeStruct(hidden.shape...  2.34 us

profile of v5, /device:TPU:0, one launch (start us, length us, event | category | flops | bytes accessed | tf_op | source)
XLA Modules:
  0.0 56.4 jit_solution(8788446280871871645)
XLA Ops:
  0.6 53.4 %shard_map.95 = (bf16[1440,128]{1,0:T(8,128)(2,1)}, bf16[8,72,768]{2,1,0:T(8,128)(2,1)}) custom-call(bf16[128,1024]{1,0:T(8,128)(2,1)} %q_hbm.1, bf16[128,128]{1,0:T(8,128)(2,1)} %k_hbm.1, bf16[128,128]{1,0:T(8,128)(2,1)} %v_hbm.1, bf16[2880,128]{1,0:T(8,128)(2,1)} %bitcast.8, s32[4,128]{1,0:T(4,128)} %bitcast.9, f32[2880]{0:T(1024)} %gain_ref.1, ...), custom_call_target="tpu_custom_call" | custom-call | tf_op jit(solution)/shard_map/pallas_call | solution.py:937
  54.0 2.3 %shard_map.96 = (bf16[1440,128]{1,0:T(8,128)(2,1)}, bf16[8,72,768]{2,1,0:T(8,128)(2,1)}) custom-call(bf16[1440,128]{1,0:T(8,128)(2,1)} %get-tuple-element.6.hid_in, bf16[8,72,768]{2,1,0:T(8,128)(2,1)} %get-tuple-element.7.act_in), custom_call_target="tpu_custom_call" | custom-call | tf_op jit(solution)/shard_map/pallas_call | solution.py:905

commit v6 on v5

--- a/solution.py
+++ b/solution.py
@@ -733,14 +733,11 @@
         return (owner >= 0) & (owner < length) & (step + 1 - up > 0)
 
     def each(step, action):
-        def one(up, carry):
+        for up in range(2):
+
             @pl.when(exists(step, up))
-            def _():
+            def _(up=up):
                 action(owner_of(step, up), up)
-
-            return carry
-
-        lax.fori_loop(0, 2, one, 0)
 
     def meet(owner, index):
         y_copy(owner, index).wait_recv()

time: 56.6 us -> 56.4 us (level)
  no operation moved by 1% of the time
where the time goes in v6:
time: 56.4 us; the launch traced here: 56.2 us
  Pallas kernels  55.5 us (98%)
  between operations  0.64 us (1%)
    pallas_call x1, Pallas kernels, along_line(): pl.pallas_call(functools.partial(line_kernel, count, cap, reach, late), o...  53.2 us
    pallas_call x1, Pallas kernels, placed(): pl.pallas_call(place_kernel, out_shape=(jax.ShapeDtypeStruct(hidden.shape...  2.34 us

profile of v6, /device:TPU:0, one launch (start us, length us, event | category | flops | bytes accessed | tf_op | source)
XLA Modules:
  0.0 56.2 jit_solution(17215979161519145187)
XLA Ops:
  0.6 53.2 %shard_map.95 = (bf16[1440,128]{1,0:T(8,128)(2,1)}, bf16[8,72,768]{2,1,0:T(8,128)(2,1)}) custom-call(bf16[128,1024]{1,0:T(8,128)(2,1)} %q_hbm.1, bf16[128,128]{1,0:T(8,128)(2,1)} %k_hbm.1, bf16[128,128]{1,0:T(8,128)(2,1)} %v_hbm.1, bf16[2880,128]{1,0:T(8,128)(2,1)} %bitcast.8, s32[4,128]{1,0:T(4,128)} %bitcast.9, f32[2880]{0:T(1024)} %gain_ref.1, ...), custom_call_target="tpu_custom_call" | custom-call | tf_op jit(solution)/shard_map/pallas_call | solution.py:934
  53.8 2.3 %shard_map.96 = (bf16[1440,128]{1,0:T(8,128)(2,1)}, bf16[8,72,768]{2,1,0:T(8,128)(2,1)}) custom-call(bf16[1440,128]{1,0:T(8,128)(2,1)} %get-tuple-element.6.hid_in, bf16[8,72,768]{2,1,0:T(8,128)(2,1)} %get-tuple-element.7.act_in), custom_call_target="tpu_custom_call" | custom-call | tf_op jit(solution)/shard_map/pallas_call | solution.py:902
